TPU v7x, 32 devices: a whole 2x2x4 slice. The times are simulated.
32 devices in a mesh: items: 8 (over y, x, core), seq: 4 (over z).
Axes of the slice: x: 2, y: 2, z: 4, core: 2. Of those that a mesh axis runs over, the one named last changes fastest.
Arguments:
- tokens: bfloat16 [24, 400, 768], P('items', 'seq'), may hold values from -6 to 6
- cotangent: bfloat16 [24, 400, 768], P('items', 'seq'), may hold values from -6 to 6
- ln1_gain: bfloat16 [768], replicated, may hold values from 0.099609375 to 1.8984375
- ln1_shift: bfloat16 [768], replicated, may hold values from -3 to 3
- w_query: bfloat16 [768, 768], replicated, may hold values from -0.21875 to 0.21875
- b_query: bfloat16 [768], replicated, may hold values from -3 to 3
- w_key: bfloat16 [768, 768], replicated, may hold values from -0.21875 to 0.21875
- w_value: bfloat16 [768, 768], replicated, may hold values from -0.21875 to 0.21875
- b_value: bfloat16 [768], replicated, may hold values from -3 to 3
- w_out: bfloat16 [768, 768], replicated, may hold values from -3.5 to 3.5
- b_out: bfloat16 [768], replicated, may hold values from -3 to 3
- ln2_gain: bfloat16 [768], replicated, may hold values from 0.099609375 to 1.8984375
- ln2_shift: bfloat16 [768], replicated, may hold values from -3 to 3
- w_inner: bfloat16 [768, 3072], replicated, may hold values from -0.21875 to 0.21875
- b_inner: bfloat16 [3072], replicated, may hold values from -3 to 3
- w_outer: bfloat16 [3072, 768], replicated, may hold values from -0.109375 to 0.109375
- b_outer: bfloat16 [768], replicated, may hold values from -3 to 3
- key_valid: int32 [24, 400], P('items'), may hold values from 0 to 1, as said below
Outputs:
- out_tokens: bfloat16 [24, 400, 768], P('items', 'seq')
- grad_tokens: bfloat16 [24, 400, 768], P('items', 'seq')
- grad_ln1_gain: float32 [768], replicated
- grad_ln1_shift: float32 [768], replicated
- grad_w_query: float32 [768, 768], replicated
- grad_b_query: float32 [768], replicated
- grad_w_key: float32 [768, 768], replicated
- grad_w_value: float32 [768, 768], replicated
- grad_b_value: float32 [768], replicated
- grad_w_out: float32 [768, 768], replicated
- grad_b_out: float32 [768], replicated
- grad_ln2_gain: float32 [768], replicated
- grad_ln2_shift: float32 [768], replicated
- grad_w_inner: float32 [768, 3072], replicated
- grad_b_inner: float32 [3072], replicated
- grad_w_outer: float32 [3072, 768], replicated
- grad_b_outer: float32 [768], replicated
Inputs may be any that keep to these rules, and one draw needn't show every extreme that they name: `key_valid`: in each item the ones come first and the zeros last; an item has 1 to 3 zeros, and some item has exactly 3.
All inputs are finite; a program needn't handle non-finite values.
Results may differ from a plain program's by a relative error of at most 0.012.
The roundings to bfloat16 on the way count: a program that leaves them out, or rounds other values in their place, can miss the bound.
Values may be sent and summed in bfloat16 or wider, within the bound.
No kernel may reach another device: no remote copies, remote signals or barrier semaphores. Data moves between devices by JAX's collectives and lax.ppermute only.
A program may use at most 192 MiB of HBM per device.

v0:
```python
import jax
import jax.numpy as jnp
from jax import lax
from jax.sharding import PartitionSpec as P

D = 768
HEADS = 12
HEAD_DIM = 64
FF = 3072
EPSILON = 1e-06
MASKED = -1000000000.0


def norm_rows(values, gain, shift):
    center = values - jnp.mean(values, axis=-1, keepdims=True)
    spread = jnp.mean(center * center, axis=-1, keepdims=True)
    return center * lax.rsqrt(spread + EPSILON) * gain + shift


def gelu_exact(values):
    return jax.nn.gelu(values, approximate=False)


def flat_rows(values):
    return values.reshape(-1, values.shape[-1])


def tall_dot(left, right):
    return jnp.einsum(
        "ti,tj->ij", flat_rows(left), flat_rows(right), preferred_element_type=jnp.float32
    )


def wide_dot(left, weight):
    return jnp.dot(flat_rows(left), weight, preferred_element_type=jnp.float32)


def back_dot(grads, weight):
    return jnp.einsum("tj,ij->ti", flat_rows(grads), weight, preferred_element_type=jnp.float32)


def column_sum(values):
    return jnp.sum(flat_rows(values.astype(jnp.float32)), axis=0)


def attend_scores(queries, keysets, usable, factor):
    scores = (
        jnp.einsum("bqhd,bkhd->bhqk", queries, keysets, preferred_element_type=jnp.float32) * factor
    )
    return jnp.where(usable[:, None, None, :] > 0, scores, MASKED)


def local(
    tokens,
    cotangent,
    ln1_gain,
    ln1_shift,
    w_query,
    b_query,
    w_key,
    w_value,
    b_value,
    w_out,
    b_out,
    ln2_gain,
    ln2_shift,
    w_inner,
    b_inner,
    w_outer,
    b_outer,
    key_valid,
):
    groups = lax.axis_size("seq")
    item_count, row_count, model_width = tokens.shape
    length = row_count * groups
    heads_here = HEADS // groups
    factor = HEAD_DIM ** (-0.5)
    token_shape = (item_count, row_count, model_width)
    head_shape = (item_count, length, heads_here, HEAD_DIM)
    inputs = tokens.astype(jnp.float32)
    normed, first_pull = jax.vjp(
        norm_rows, inputs, ln1_gain.astype(jnp.float32), ln1_shift.astype(jnp.float32)
    )
    normed_low = normed.astype(jnp.bfloat16)
    query = (
        (wide_dot(normed_low, w_query) + b_query.astype(jnp.float32))
        .astype(jnp.bfloat16)
        .reshape(token_shape)
    )
    keyset = wide_dot(normed_low, w_key).astype(jnp.bfloat16).reshape(token_shape)
    values = (
        (wide_dot(normed_low, w_value) + b_value.astype(jnp.float32))
        .astype(jnp.bfloat16)
        .reshape(token_shape)
    )
    query_heads, key_heads, value_heads = (
        lax.all_to_all(query, "seq", split_axis=2, concat_axis=1, tiled=True),
        lax.all_to_all(keyset, "seq", split_axis=2, concat_axis=1, tiled=True),
        lax.all_to_all(values, "seq", split_axis=2, concat_axis=1, tiled=True),
    )
    query_four = query_heads.reshape(head_shape)
    key_four = key_heads.reshape(head_shape)
    value_four = value_heads.reshape(head_shape)
    scores = attend_scores(query_four, key_four, key_valid, factor)
    row_top = jnp.max(scores, axis=-1, keepdims=True)
    weights = jnp.exp(scores - row_top)
    totals = jnp.sum(weights, axis=-1, keepdims=True)
    logsum = row_top + jnp.log(totals)
    probs_low = (weights / totals).astype(jnp.bfloat16)
    mixed = jnp.einsum("bhqk,bkhd->bqhd", probs_low, value_four, preferred_element_type=jnp.float32)
    mixed = mixed.astype(jnp.bfloat16).reshape(item_count, length, heads_here * HEAD_DIM)
    mixed_tokens = lax.all_to_all(mixed, "seq", split_axis=1, concat_axis=2, tiled=True)
    hidden = inputs + wide_dot(mixed_tokens, w_out).reshape(token_shape) + b_out.astype(jnp.float32)
    normed_two, second_pull = jax.vjp(
        norm_rows, hidden, ln2_gain.astype(jnp.float32), ln2_shift.astype(jnp.float32)
    )
    normed_two_low = normed_two.astype(jnp.bfloat16)
    inner = (wide_dot(normed_two_low, w_inner) + b_inner.astype(jnp.float32)).reshape(
        item_count, row_count, FF
    )
    active, gelu_pull = jax.vjp(gelu_exact, inner)
    active_low = active.astype(jnp.bfloat16)
    result = (
        hidden + wide_dot(active_low, w_outer).reshape(token_shape) + b_outer.astype(jnp.float32)
    )
    out_tokens = result.astype(jnp.bfloat16)
    grad_w_outer = tall_dot(active_low, cotangent)
    grad_b_outer = column_sum(cotangent)
    d_active = back_dot(cotangent, w_outer).reshape(item_count, row_count, FF)
    (d_inner,) = gelu_pull(d_active)
    d_inner_low = d_inner.astype(jnp.bfloat16)
    grad_w_inner = tall_dot(normed_two_low, d_inner_low)
    grad_b_inner = column_sum(d_inner_low)
    d_normed_two = back_dot(d_inner_low, w_inner).reshape(token_shape)
    d_hidden_part, grad_ln2_gain, grad_ln2_shift = second_pull(d_normed_two)
    d_hidden = cotangent.astype(jnp.float32) + d_hidden_part
    grad_b_out = column_sum(d_hidden)
    d_hidden_low = d_hidden.astype(jnp.bfloat16)
    grad_w_out = tall_dot(mixed_tokens, d_hidden_low)
    d_mixed = back_dot(d_hidden_low, w_out).astype(jnp.bfloat16).reshape(token_shape)
    d_mixed_heads = lax.all_to_all(d_mixed, "seq", split_axis=2, concat_axis=1, tiled=True)
    d_mixed_four = d_mixed_heads.reshape(head_shape)
    scores = attend_scores(query_four, key_four, key_valid, factor)
    probs = jnp.exp(scores - logsum)
    d_value = jnp.einsum(
        "bhqk,bqhd->bkhd",
        probs.astype(jnp.bfloat16),
        d_mixed_four,
        preferred_element_type=jnp.float32,
    )
    d_probs = jnp.einsum(
        "bqhd,bkhd->bhqk", d_mixed_four, value_four, preferred_element_type=jnp.float32
    )
    weighted = jnp.sum(probs * d_probs, axis=-1, keepdims=True)
    d_scores = (probs * (d_probs - weighted)).astype(jnp.bfloat16)
    d_query = (
        jnp.einsum("bhqk,bkhd->bqhd", d_scores, key_four, preferred_element_type=jnp.float32)
        * factor
    )
    d_key = (
        jnp.einsum("bhqk,bqhd->bkhd", d_scores, query_four, preferred_element_type=jnp.float32)
        * factor
    )
    flat_shape = (item_count, length, heads_here * HEAD_DIM)
    d_query = d_query.astype(jnp.bfloat16).reshape(flat_shape)
    d_key = d_key.astype(jnp.bfloat16).reshape(flat_shape)
    d_value = d_value.astype(jnp.bfloat16).reshape(flat_shape)
    d_query_tok, d_key_tok, d_value_tok = (
        lax.all_to_all(d_query, "seq", split_axis=1, concat_axis=2, tiled=True),
        lax.all_to_all(d_key, "seq", split_axis=1, concat_axis=2, tiled=True),
        lax.all_to_all(d_value, "seq", split_axis=1, concat_axis=2, tiled=True),
    )
    grad_w_query = tall_dot(normed_low, d_query_tok)
    grad_b_query = column_sum(d_query_tok)
    grad_w_key = tall_dot(normed_low, d_key_tok)
    grad_w_value = tall_dot(normed_low, d_value_tok)
    grad_b_value = column_sum(d_value_tok)
    d_normed = (
        back_dot(d_query_tok, w_query) + back_dot(d_key_tok, w_key) + back_dot(d_value_tok, w_value)
    )
    d_input_part, grad_ln1_gain, grad_ln1_shift = first_pull(d_normed.reshape(token_shape))
    grad_tokens = (d_hidden + d_input_part).astype(jnp.bfloat16)
    smalls = jnp.concatenate(
        [
            grad_ln1_gain,
            grad_ln1_shift,
            grad_b_query,
            grad_b_value,
            grad_b_out,
            grad_ln2_gain,
            grad_ln2_shift,
            grad_b_outer,
            grad_b_inner,
        ]
    )
    flat_query = grad_w_query.reshape(-1)
    flat_key = grad_w_key.reshape(-1)
    flat_value = grad_w_value.reshape(-1)
    flat_out = grad_w_out.reshape(-1)
    flat_inner = grad_w_inner.reshape(-1)
    flat_outer = grad_w_outer.reshape(-1)
    shares = (
        lax.psum_scatter(flat_query, ("items", "seq"), scatter_dimension=0, tiled=True),
        lax.psum_scatter(flat_key, ("items", "seq"), scatter_dimension=0, tiled=True),
        lax.psum_scatter(flat_value, ("items", "seq"), scatter_dimension=0, tiled=True),
        lax.psum_scatter(flat_out, ("items", "seq"), scatter_dimension=0, tiled=True),
        lax.psum_scatter(flat_inner, ("items", "seq"), scatter_dimension=0, tiled=True),
        lax.psum_scatter(flat_outer, ("items", "seq"), scatter_dimension=0, tiled=True),
        lax.psum_scatter(smalls, ("items", "seq"), scatter_dimension=0, tiled=True),
    )
    summed = (
        lax.all_gather(shares[0].astype(jnp.bfloat16), ("items", "seq"), axis=0, tiled=True).astype(
            jnp.float32
        ),
        lax.all_gather(shares[1].astype(jnp.bfloat16), ("items", "seq"), axis=0, tiled=True).astype(
            jnp.float32
        ),
        lax.all_gather(shares[2].astype(jnp.bfloat16), ("items", "seq"), axis=0, tiled=True).astype(
            jnp.float32
        ),
        lax.all_gather(shares[3].astype(jnp.bfloat16), ("items", "seq"), axis=0, tiled=True).astype(
            jnp.float32
        ),
        lax.all_gather(shares[4].astype(jnp.bfloat16), ("items", "seq"), axis=0, tiled=True).astype(
            jnp.float32
        ),
        lax.all_gather(shares[5].astype(jnp.bfloat16), ("items", "seq"), axis=0, tiled=True).astype(
            jnp.float32
        ),
        lax.all_gather(shares[6].astype(jnp.bfloat16), ("items", "seq"), axis=0, tiled=True).astype(
            jnp.float32
        ),
    )
    sum_query, sum_key, sum_value, sum_out, sum_inner, sum_outer, sum_small = summed
    width = D
    return (
        out_tokens,
        grad_tokens,
        sum_small[0:width],
        sum_small[width : 2 * width],
        sum_query.reshape(D, D),
        sum_small[2 * width : 3 * width],
        sum_key.reshape(D, D),
        sum_value.reshape(D, D),
        sum_small[3 * width : 4 * width],
        sum_out.reshape(D, D),
        sum_small[4 * width : 5 * width],
        sum_small[5 * width : 6 * width],
        sum_small[6 * width : 7 * width],
        sum_inner.reshape(D, FF),
        sum_small[8 * width : 8 * width + FF],
        sum_outer.reshape(FF, D),
        sum_small[7 * width : 8 * width],
    )


def solution(mesh):
    in_specs = (
        P("items", "seq", None),
        P("items", "seq", None),
        P(),
        P(),
        P(),
        P(),
        P(),
        P(),
        P(),
        P(),
        P(),
        P(),
        P(),
        P(),
        P(),
        P(),
        P(),
        P("items", None),
    )
    out_specs = (
        P("items", "seq", None),
        P("items", "seq", None),
        P(),
        P(),
        P(),
        P(),
        P(),
        P(),
        P(),
        P(),
        P(),
        P(),
        P(),
        P(),
        P(),
        P(),
        P(),
    )
    return jax.shard_map(local, mesh=mesh, in_specs=in_specs, out_specs=out_specs, check_vma=False)
```

profile of v0, /device:TPU:0, one launch (start us, length us, event | category | flops | bytes accessed | tf_op | source)
XLA Modules:
  0.0 1186.7 jit_solution(8166704738698876618)
XLA Ops:
  16.3 6.3 all-to-all-start
  25.9 16.9 %all-to-all-done = bf16[3,100,768]{1,0,2:T(4,128)(2,1)S(1)} async-done(((bf16[3,100,768]{1,0,2:T(4,128)(2,1)}), bf16[3,100,768]{1,0,2:T(4,128)(2,1)S(1)}, u32[]{:S(2)}, u32[]{:S(2)}) %all-to-all-start) | async-done | bytes 460832 | tf_op jit(solution)/shard_map/all_to_all | solution.py:99
  52.9 13.0 %all-to-all-done.1 = bf16[3,100,768]{1,0,2:T(4,128)(2,1)S(1)} async-done(((bf16[3,100,768]{1,0,2:T(4,128)(2,1)}), bf16[3,100,768]{1,0,2:T(4,128)(2,1)S(1)}, u32[]{:S(2)}, u32[]{:S(2)}) %all-to-all-start.1) | async-done | bytes 460832 | tf_op jit(solution)/shard_map/all_to_all | solution.py:97
  65.9 4.2 all-to-all-start.2
  74.1 15.8 %all-to-all-done.2 = bf16[3,100,768]{1,0,2:T(4,128)(2,1)} async-done(((bf16[3,100,768]{1,0,2:T(4,128)(2,1)}), bf16[3,100,768]{1,0,2:T(4,128)(2,1)}, u32[]{:S(2)}, u32[]{:S(2)}) %all-to-all-start.2) | async-done | bytes 460832 | tf_op jit(solution)/shard_map/all_to_all | solution.py:98
  107.3 20.2 %all-to-all-done.3 = bf16[3,400,192]{2,0,1:T(4,128)(2,1)S(1)} async-done(((bf16[3,400,192]{2,0,1:T(4,128)(2,1)}), bf16[3,400,192]{2,0,1:T(4,128)(2,1)S(1)}, u32[]{:S(2)}, u32[]{:S(2)}) %all-to-all-start.3) | async-done | bytes 460832 | tf_op jit(solution)/shard_map/all_to_all | solution.py:112
  137.3 13.2 %negate_multiply_fusion = (f32[300,3072]{1,0:T(8,128)}, bf16[300,3072]{1,0:T(8,128)(2,1)}, f32[300,3072]{1,0:T(8,128)}) fusion(f32[3072]{0:T(1024)S(1)} %convert_element_type.162, bf16[300,768]{1,0:T(8,128)(2,1)} %reshape.289, bf16[768,3072]{1,0:T(8,128)(2,1)} %param.31), kind=kOutput, calls=%fused_computation.49 | convolution fusion | flops 1476403200 | bytes 14407680 | tf_op jit(solution)/shard_map/dot_general | solution.py:35
  158.1 13.9 %convert_reduce_fusion = (f32[3072]{0:T(1024)}, bf16[3,100,3072]{2,1,0:T(8,128)(2,1)S(1)}) fusion(f32[3,100,3072]{2,1,0:T(8,128)} %mul.183, f32[3,100,3072]{2,1,0:T(8,128)} %mul.179, bf16[3,100,768]{2,1,0:T(8,128)(2,1)} %param.19, bf16[3072,768]{1,0:T(8,128)(2,1)} %param.33), kind=kOutput, calls=%fused_computation.20 | convolution fusion | flops 1481008128 | bytes 14407680 | tf_op jit(solution)/shard_map/tj,ij->ti/dot_general | solution.py:39
  172.0 5.7 multiply_reduce_fusion.1
  185.2 4.7 all-to-all-start.4
  189.9 14.2 %convolution_bitcast_fusion = f32[3072,768]{1,0:T(8,128)} fusion(bf16[3,100,768]{2,1,0:T(8,128)(2,1)S(1)} %copy-done.24, f32[3,100,3072]{2,1,0:T(8,128)} %mul.179, f32[3,100,3072]{2,1,0:T(8,128)} %mul.183), kind=kOutput, calls=%fused_computation.8 | convolution fusion | flops 1472716800 | bytes 17270784 | tf_op jit(solution)/shard_map/ti,tj->ij/dot_general | solution.py:29
  215.4 5.5 multiply_reduce_fusion
  221.0 4.6 multiply_convert_fusion
  229.6 5.2 all-to-all-start.5
  234.8 4.4 convolution_bitcast_fusion.1
  239.2 5.9 copy.146
  245.1 10.8 reshape.316
  255.9 4.1 fusion.36
  262.2 5.1 all-to-all-start.6
  267.3 5.1 fusion.38
  279.1 7.6 all-to-all-done.6
  301.1 9.4 all-to-all-done.7
  357.3 460.4 %all-reduce.10 = (bf16[9216]{0:T(1024)(128)(2,1)}, bf16[589824]{0:T(1024)(128)(2,1)}, bf16[589824]{0:T(1024)(128)(2,1)}, bf16[589824]{0:T(1024)(128)(2,1)}, bf16...) all-reduce(f32[9216]{0:T(1024)} %constant_dynamic-update-slice_fusi, ...), channel_id=2, replica_groups=mesh['items'=8,'seq'=4] {'items','seq'}, use_global_device_ids=true, to_apply=%region_20.21.clone | all-reduce | flops 7087104 | bytes 42522624
  829.7 5.4 fusion.47
  836.0 37.5 %all-reduce = bf16[9216]{0:T(1024)(128)(2,1)S(1)} all-reduce(bf16[9216]{0:T(1024)(128)(2,1)S(1)} %dynamic-update-slice), channel_id=1, replica_groups=mesh['items'=8,'seq'=4] {'items','seq'}, use_global_device_ids=true, to_apply=%add | all-reduce | flops 9216 | bytes 36864
  878.1 49.6 %all-gather.9.cloned.1.call-done = bf16[589824]{0:T(1024)(128)(2,1)} async-done(((bf16[18432]{0:T(1024)(128)(2,1)}), bf16[589824]{0:T(1024)(128)(2,1)}) %all-gather.9.cloned.1.call-update) | async-done | bytes 1179664 | tf_op jit(solution)/shard_map/all_gather | solution.py:215
  931.0 52.4 %all-gather.11.cloned.1.call-done = bf16[589824]{0:T(1024)(128)(2,1)} async-done(((bf16[18432]{0:T(1024)(128)(2,1)}), bf16[589824]{0:T(1024)(128)(2,1)}) %all-gather.11.cloned.1.call-update) | async-done | bytes 1179664 | tf_op jit(solution)/shard_map/all_gather | solution.py:218
  986.8 52.3 %all-gather.13.cloned.1.call-done = bf16[589824]{0:T(1024)(128)(2,1)} async-done(((bf16[18432]{0:T(1024)(128)(2,1)}), bf16[589824]{0:T(1024)(128)(2,1)}) %all-gather.13.cloned.1.call-update) | async-done | bytes 1179664 | tf_op jit(solution)/shard_map/all_gather | solution.py:221
  1042.4 62.4 %all-gather.15.cloned.1.call-done = bf16[2359296]{0:T(1024)(128)(2,1)} async-done(((bf16[73728]{0:T(1024)(128)(2,1)}), bf16[2359296]{0:T(1024)(128)(2,1)}) %all-gather.15.cloned.1.call-update) | async-done | bytes 4718608 | tf_op jit(solution)/shard_map/all_gather | solution.py:224
  1104.8 8.7 reshape.328
  1113.6 55.8 %all-gather.17.cloned.1.call-done = bf16[2359296]{0:T(1024)(128)(2,1)} async-done(((bf16[73728]{0:T(1024)(128)(2,1)}), bf16[2359296]{0:T(1024)(128)(2,1)}) %all-gather.17.cloned.1.call-update) | async-done | bytes 4718608 | tf_op jit(solution)/shard_map/all_gather | solution.py:227
  1169.4 10.0 reshape.330
  (228 shorter events, 181.1 us)
Async XLA Ops:
  13.7 32.6 %copy-start.9 = (bf16[300,768]{1,0:T(8,128)(2,1)}, bf16[300,768]{1,0:T(8,128)(2,1)S(1)}, u32[]{:S(2)}) copy-start(bf16[300,768]{1,0:T(8,128)(2,1)S(1)} %reshape.281) | copy-start | bytes 1382404
  16.3 26.5 %all-to-all-start = ((bf16[3,100,768]{1,0,2:T(4,128)(2,1)}), bf16[3,100,768]{1,0,2:T(4,128)(2,1)S(1)}, u32[]{:S(2)}, u32[]{:S(2)}) async-start(bf16[3,100,768]{1,0,2:T(4,128)(2,1)} %copy.94), calls=%async_computation | async-start | bytes 1572864 | tf_op jit(solution)/shard_map/all_to_all | solution.py:99
  25.9 44.3 %copy-start.39 = (s32[3,400]{1,0:T(4,128)S(1)}, s32[3,400]{1,0:T(4,128)}, u32[]{:S(2)}) copy-start(s32[3,400]{1,0:T(4,128)} %param.35) | copy-start | bytes 14404
  42.8 23.1 %all-to-all-start.1 = ((bf16[3,100,768]{1,0,2:T(4,128)(2,1)}), bf16[3,100,768]{1,0,2:T(4,128)(2,1)S(1)}, u32[]{:S(2)}, u32[]{:S(2)}) async-start(bf16[3,100,768]{1,0,2:T(4,128)(2,1)} %copy.97), calls=%async_computation.1 | async-start | bytes 1572864 | tf_op jit(solution)/shard_map/all_to_all | solution.py:97
  65.9 23.9 %all-to-all-start.2 = ((bf16[3,100,768]{1,0,2:T(4,128)(2,1)}), bf16[3,100,768]{1,0,2:T(4,128)(2,1)}, u32[]{:S(2)}, u32[]{:S(2)}) async-start(bf16[3,100,768]{1,0,2:T(4,128)(2,1)} %copy.100), calls=%async_computation.2 | async-start | bytes 1572864 | tf_op jit(solution)/shard_map/all_to_all | solution.py:98
  73.2 24.8 %copy-start.20 = (bf16[3,400,3,64]{1,3,2,0:T(8,128)(2,1)}, bf16[3,400,3,64]{1,3,2,0:T(8,128)(2,1)S(1)}, u32[]{:S(2)}) copy-start(bf16[3,400,3,64]{1,3,2,0:T(8,128)(2,1)S(1)} %reshape.283) | copy-start | bytes 1382404
  98.0 9.2 copy-start.42
  98.0 9.3 copy-start.40
  98.0 9.3 copy-start.43
  98.0 9.3 copy-start.44
  101.2 30.9 %copy-start.3 = (bf16[3,100,768]{2,1,0:T(8,128)(2,1)S(1)}, bf16[3,100,768]{2,1,0:T(8,128)(2,1)}, u32[]{:S(2)}) copy-start(bf16[3,100,768]{2,1,0:T(8,128)(2,1)} %param.18) | copy-start | bytes 1382404
  103.5 24.0 %all-to-all-start.3 = ((bf16[3,400,192]{2,0,1:T(4,128)(2,1)}), bf16[3,400,192]{2,0,1:T(4,128)(2,1)S(1)}, u32[]{:S(2)}, u32[]{:S(2)}) async-start(bf16[3,400,192]{2,0,1:T(4,128)(2,1)} %copy.104), calls=%async_computation.3 | async-start | bytes 1638400 | tf_op jit(solution)/shard_map/all_to_all | solution.py:112
  107.3 113.7 %copy-start.28 = (f32[3,3,400]{2,1,0:T(4,128)}, f32[3,3,400]{2,1,0:T(4,128)S(1)}, u32[]{:S(2)}) copy-start(f32[3,3,400]{2,1,0:T(4,128)S(1)} %log_add_fusion) | copy-start | bytes 43204
  134.2 43.5 %copy-start.7 = (f32[3,100,768]{2,1,0:T(8,128)}, f32[3,100,768]{2,1,0:T(8,128)S(1)}, u32[]{:S(2)}) copy-start(f32[3,100,768]{2,1,0:T(8,128)S(1)} %get-tuple-element.48) | copy-start | bytes 2764804
  179.3 10.7 copy-start.24
  185.2 26.1 %all-to-all-start.4 = ((bf16[3,100,768]{1,0,2:T(4,128)(2,1)}), bf16[3,100,768]{1,0,2:T(4,128)(2,1)}, u32[]{:S(2)}, u32[]{:S(2)}) async-start(bf16[3,100,768]{1,0,2:T(4,128)(2,1)} %copy.107), calls=%async_computation.4 | async-start | bytes 1572864 | tf_op jit(solution)/shard_map/all_to_all | solution.py:141
  189.9 14.3 %copy-start.16 = (bf16[3,100,4,192]{3,2,1,0:T(4,128)(2,1)S(1)}, bf16[3,100,4,192]{3,2,1,0:T(4,128)(2,1)}, u32[]{:S(2)}) copy-start(bf16[3,100,4,192]{3,2,1,0:T(4,128)(2,1)} %copy-done.15) | copy-start | bytes 1382404
  229.6 32.6 %all-to-all-start.5 = ((bf16[3,400,192]{2,0,1:T(4,128)(2,1)}), bf16[3,400,192]{2,0,1:T(4,128)(2,1)S(1)}, u32[]{:S(2)}, u32[]{:S(2)}) async-start(bf16[3,400,192]{2,0,1:T(4,128)(2,1)} %copy.111), calls=%async_computation.5 | async-start | bytes 1638400 | tf_op jit(solution)/shard_map/all_to_all | solution.py:169
  255.9 11.4 copy-start.29
  262.2 11.6 copy-start.11
  262.2 24.5 %all-to-all-start.6 = ((bf16[3,400,192]{2,0,1:T(4,128)(2,1)}), bf16[3,400,192]{2,0,1:T(4,128)(2,1)}, u32[]{:S(2)}, u32[]{:S(2)}) async-start(bf16[3,400,192]{2,0,1:T(4,128)(2,1)} %copy.115), calls=%async_computation.6 | async-start | bytes 1638400 | tf_op jit(solution)/shard_map/all_to_all | solution.py:170
  286.7 23.8 %all-to-all-start.7 = ((bf16[3,400,192]{2,0,1:T(4,128)(2,1)}), bf16[3,400,192]{2,0,1:T(4,128)(2,1)S(1)}, u32[]{:S(2)}, u32[]{:S(2)}) async-start(bf16[3,400,192]{2,0,1:T(4,128)(2,1)} %copy.119), calls=%async_computation.7 | async-start | bytes 1638400 | tf_op jit(solution)/shard_map/all_to_all | solution.py:171
  290.2 584.5 %all-gather.7.cloned.1.call-start = ((), (), s32[]{:S(2)}) async-start(), calls=%async_computation.8 | async-start | bytes 1216512 | tf_op jit(solution)/shard_map/all_gather | solution.py:212
  322.6 14.8 %copy-start.38 = (f32[768]{0:T(1024)S(1)}, f32[768]{0:T(1024)}, u32[]{:S(2)}) copy-start(f32[768]{0:T(1024)} %get-tuple-element.19) | copy-start | bytes 9220
  322.6 26.5 %copy-start.5 = (f32[768,768]{1,0:T(8,128)S(1)}, f32[768,768]{1,0:T(8,128)}, u32[]{:S(2)}) copy-start(f32[768,768]{1,0:T(8,128)} %fusion.75) | copy-start | bytes 7077892
  357.3 469.6 %copy-start.45 = (bf16[768]{0:T(1024)(128)(2,1)S(1)}, bf16[768]{0:T(1024)(128)(2,1)}, u32[]{:S(2)}) copy-start(bf16[768]{0:T(1024)(128)(2,1)} %param.34) | copy-start | bytes 4612
  817.7 12.0 %copy-start.8 = (f32[3,100,768]{2,1,0:T(8,128)S(1)}, f32[3,100,768]{2,1,0:T(8,128)}, u32[]{:S(2)}) copy-start(f32[3,100,768]{2,1,0:T(8,128)} %copy-done.7) | copy-start | bytes 2764804
  819.2 108.5 %all-gather.9.cloned.1.call-start = ((), (), s32[]{:S(2)}) async-start(), calls=%async_computation.9 | async-start | bytes 1216512 | tf_op jit(solution)/shard_map/all_gather | solution.py:215
  820.6 162.8 %all-gather.11.cloned.1.call-start = ((), (), s32[]{:S(2)}) async-start(), calls=%async_computation.10 | async-start | bytes 1216512 | tf_op jit(solution)/shard_map/all_gather | solution.py:218
  822.1 216.9 %all-gather.13.cloned.1.call-start = ((), (), s32[]{:S(2)}) async-start(), calls=%async_computation.11 | async-start | bytes 1216512 | tf_op jit(solution)/shard_map/all_gather | solution.py:221
  823.6 281.3 %all-gather.15.cloned.1.call-start = ((), (), s32[]{:S(2)}) async-start(), calls=%async_computation.12 | async-start | bytes 4866048 | tf_op jit(solution)/shard_map/all_gather | solution.py:224
  825.2 344.2 %all-gather.17.cloned.1.call-start = ((), (), s32[]{:S(2)}) async-start(), calls=%async_computation.13 | async-start | bytes 4866048 | tf_op jit(solution)/shard_map/all_gather | solution.py:227
  (28 other events, 110.1 us)
Sparse Core Ops, SparseCore 0:
  819.3 52.1 all-gather.6
  874.9 52.7 all-gather.8
  930.5 52.9 all-gather.10
  986.1 52.8 all-gather.12
  1042.3 62.5 all-gather.14
  1107.5 61.8 all-gather.16
where the time goes:
time: 1200 us; the launch traced here: 1190 us
  blocking collectives  498 us (42%)
  waiting for transfers between devices  356 us (30%)
  local copies, waits for them, and re-layouts  156 us (13%)
  matrix products  103 us (9%)
  starting transfers between devices  36.5 us (3%)
  other arithmetic  22.6 us (2%)
  between operations  15.3 us (1%)
    unnamed x2, blocking collectives  498 us
    all_gather x1, waiting for transfers between devices, local(): lax.all_gather(shares[4].astype(jnp.bfloat16), ('items', 'seq'), axis=0,...  62.4 us
    all_gather x1, waiting for transfers between devices, local(): lax.all_gather(shares[5].astype(jnp.bfloat16), ('items', 'seq'), axis=0,...  55.8 us
    all_gather x1, waiting for transfers between devices, local(): lax.all_gather(shares[2].astype(jnp.bfloat16), ('items', 'seq'), axis=0,...  52.4 us
    all_gather x1, waiting for transfers between devices, local(): lax.all_gather(shares[3].astype(jnp.bfloat16), ('items', 'seq'), axis=0,...  52.3 us
    all_gather x1, waiting for transfers between devices, local(): lax.all_gather(shares[1].astype(jnp.bfloat16), ('items', 'seq'), axis=0,...  49.6 us
    unnamed x110, local copies, waits for them, and re-layouts  31.7 us
    dot_general x6, matrix products, tall_dot(): jnp.einsum('ti,tj->ij', flat_rows(left), flat_rows(right), preferred_elem...  28.5 us
  transfers between devices with their start and end apart: 14, of which 11 were waited for; matrix products, arithmetic and copies ran while one was open for 11% of the time, Pallas kernels for 0%

commit v1 on v0

--- a/solution.py
+++ b/solution.py
@@ -109,7 +109,9 @@
     probs_low = (weights / totals).astype(jnp.bfloat16)
     mixed = jnp.einsum("bhqk,bkhd->bqhd", probs_low, value_four, preferred_element_type=jnp.float32)
     mixed = mixed.astype(jnp.bfloat16).reshape(item_count, length, heads_here * HEAD_DIM)
-    mixed_tokens = lax.all_to_all(mixed, "seq", split_axis=1, concat_axis=2, tiled=True)
+    pieces = jnp.split(mixed, lax.axis_size("seq"), axis=1)
+    received = lax.all_to_all(jnp.stack(pieces), "seq", 0, 0)
+    mixed_tokens = jnp.concatenate(received, axis=2)
     hidden = inputs + wide_dot(mixed_tokens, w_out).reshape(token_shape) + b_out.astype(jnp.float32)
     normed_two, second_pull = jax.vjp(
         norm_rows, hidden, ln2_gain.astype(jnp.float32), ln2_shift.astype(jnp.float32)

time: 1200 us -> 1190 us (level)
    unnamed x110 -> x108, local copies, waits for them, and re-layouts: 31.7 us -> 30.8 us
where the time goes in v1:
time: 1190 us; the launch traced here: 1180 us
  blocking collectives  498 us (42%)
  waiting for transfers between devices  350 us (29%)
  local copies, waits for them, and re-layouts  152 us (13%)
  matrix products  102 us (9%)
  starting transfers between devices  36.5 us (3%)
  other arithmetic  24.1 us (2%)
  between operations  15.4 us (1%)
    unnamed x2, blocking collectives  498 us
    all_gather x1, waiting for transfers between devices, local(): lax.all_gather(shares[4].astype(jnp.bfloat16), ('items', 'seq'), axis=0,...  62.4 us
    all_gather x1, waiting for transfers between devices, local(): lax.all_gather(shares[5].astype(jnp.bfloat16), ('items', 'seq'), axis=0,...  55.8 us
    all_gather x1, waiting for transfers between devices, local(): lax.all_gather(shares[2].astype(jnp.bfloat16), ('items', 'seq'), axis=0,...  52.4 us
    all_gather x1, waiting for transfers between devices, local(): lax.all_gather(shares[3].astype(jnp.bfloat16), ('items', 'seq'), axis=0,...  52.3 us
    all_gather x1, waiting for transfers between devices, local(): lax.all_gather(shares[1].astype(jnp.bfloat16), ('items', 'seq'), axis=0,...  49.6 us
    unnamed x108, local copies, waits for them, and re-layouts  30.8 us
    dot_general x6, matrix products, tall_dot(): jnp.einsum('ti,tj->ij', flat_rows(left), flat_rows(right), preferred_elem...  28.5 us
  transfers between devices with their start and end apart: 14, of which 11 were waited for; matrix products, arithmetic and copies ran while one was open for 11% of the time, Pallas kernels for 0%

profile of v1, /device:TPU:0, one launch (start us, length us, event | category | flops | bytes accessed | tf_op | source)
XLA Modules:
  0.0 1178.3 jit_solution(8481112149853781753)
XLA Ops:
  16.3 6.3 all-to-all-start
  25.9 16.9 %all-to-all-done = bf16[3,100,768]{1,0,2:T(4,128)(2,1)S(1)} async-done(((bf16[3,100,768]{1,0,2:T(4,128)(2,1)}), bf16[3,100,768]{1,0,2:T(4,128)(2,1)S(1)}, u32[]{:S(2)}, u32[]{:S(2)}) %all-to-all-start) | async-done | bytes 460832 | tf_op jit(solution)/shard_map/all_to_all | solution.py:99
  52.9 13.0 %all-to-all-done.1 = bf16[3,100,768]{1,0,2:T(4,128)(2,1)S(1)} async-done(((bf16[3,100,768]{1,0,2:T(4,128)(2,1)}), bf16[3,100,768]{1,0,2:T(4,128)(2,1)S(1)}, u32[]{:S(2)}, u32[]{:S(2)}) %all-to-all-start.1) | async-done | bytes 460832 | tf_op jit(solution)/shard_map/all_to_all | solution.py:97
  65.9 4.2 all-to-all-start.2
  74.1 15.8 %all-to-all-done.2 = bf16[3,100,768]{1,0,2:T(4,128)(2,1)} async-done(((bf16[3,100,768]{1,0,2:T(4,128)(2,1)}), bf16[3,100,768]{1,0,2:T(4,128)(2,1)}, u32[]{:S(2)}, u32[]{:S(2)}) %all-to-all-start.2) | async-done | bytes 460832 | tf_op jit(solution)/shard_map/all_to_all | solution.py:98
  106.0 14.7 %all-to-all-done.3 = bf16[4,3,100,192]{2,3,1,0:T(8,128)(2,1)S(1)} async-done(((bf16[4,3,100,192]{2,3,1,0:T(8,128)(2,1)}), bf16[4,3,100,192]{2,3,1,0:T(8,128)(2,1)S(1)}, u32[]{:S(2)}, u32[]{:S(2)}) %all-to-all-start.3) | async-done | bytes 460832 | tf_op jit(solution)/shard_map/all_to_all | solution.py:113
  128.8 13.2 %negate_multiply_fusion = (f32[300,3072]{1,0:T(8,128)}, bf16[300,3072]{1,0:T(8,128)(2,1)}, f32[300,3072]{1,0:T(8,128)}) fusion(f32[3072]{0:T(1024)S(1)} %convert_element_type.162, bf16[300,768]{1,0:T(8,128)(2,1)} %reshape.288, bf16[768,3072]{1,0:T(8,128)(2,1)} %param.31), kind=kOutput, calls=%fused_computation.49 | convolution fusion | flops 1476403200 | bytes 14407680 | tf_op jit(solution)/shard_map/dot_general | solution.py:35
  149.6 13.9 %convert_reduce_fusion = (f32[3072]{0:T(1024)}, bf16[3,100,3072]{2,1,0:T(8,128)(2,1)S(1)}) fusion(f32[3,100,3072]{2,1,0:T(8,128)} %mul.183, f32[3,100,3072]{2,1,0:T(8,128)} %mul.179, bf16[3,100,768]{2,1,0:T(8,128)(2,1)} %param.19, bf16[3072,768]{1,0:T(8,128)(2,1)} %param.33), kind=kOutput, calls=%fused_computation.20 | convolution fusion | flops 1481008128 | bytes 14407680 | tf_op jit(solution)/shard_map/tj,ij->ti/dot_general | solution.py:39
  163.6 5.7 multiply_reduce_fusion.1
  176.8 4.7 all-to-all-start.4
  181.5 14.2 %convolution_bitcast_fusion = f32[3072,768]{1,0:T(8,128)} fusion(bf16[3,100,768]{2,1,0:T(8,128)(2,1)S(1)} %copy-done.23, f32[3,100,3072]{2,1,0:T(8,128)} %mul.179, f32[3,100,3072]{2,1,0:T(8,128)} %mul.183), kind=kOutput, calls=%fused_computation.8 | convolution fusion | flops 1472716800 | bytes 17270784 | tf_op jit(solution)/shard_map/ti,tj->ij/dot_general | solution.py:29
  207.0 5.5 multiply_reduce_fusion
  212.6 4.6 multiply_convert_fusion
  221.1 5.2 all-to-all-start.5
  226.4 4.4 convolution_bitcast_fusion.1
  230.7 5.9 copy.143
  236.6 10.8 reshape.314
  247.5 4.0 fusion.36
  253.8 5.1 all-to-all-start.6
  258.9 5.1 fusion.38
  270.6 7.6 all-to-all-done.6
  292.7 9.4 all-to-all-done.7
  348.8 460.4 %all-reduce.10 = (bf16[9216]{0:T(1024)(128)(2,1)}, bf16[589824]{0:T(1024)(128)(2,1)}, bf16[589824]{0:T(1024)(128)(2,1)}, bf16[589824]{0:T(1024)(128)(2,1)}, bf16...) all-reduce(f32[9216]{0:T(1024)} %constant_dynamic-update-slice_fusi, ...), channel_id=2, replica_groups=mesh['items'=8,'seq'=4] {'items','seq'}, use_global_device_ids=true, to_apply=%region_20.21.clone | all-reduce | flops 7087104 | bytes 42522624
  821.2 5.4 fusion.47
  827.5 37.5 %all-reduce = bf16[9216]{0:T(1024)(128)(2,1)S(1)} all-reduce(bf16[9216]{0:T(1024)(128)(2,1)S(1)} %dynamic-update-slice), channel_id=1, replica_groups=mesh['items'=8,'seq'=4] {'items','seq'}, use_global_device_ids=true, to_apply=%add | all-reduce | flops 9216 | bytes 36864
  869.6 49.6 %all-gather.9.cloned.1.call-done = bf16[589824]{0:T(1024)(128)(2,1)} async-done(((bf16[18432]{0:T(1024)(128)(2,1)}), bf16[589824]{0:T(1024)(128)(2,1)}) %all-gather.9.cloned.1.call-update) | async-done | bytes 1179664 | tf_op jit(solution)/shard_map/all_gather | solution.py:217
  922.6 52.4 %all-gather.11.cloned.1.call-done = bf16[589824]{0:T(1024)(128)(2,1)} async-done(((bf16[18432]{0:T(1024)(128)(2,1)}), bf16[589824]{0:T(1024)(128)(2,1)}) %all-gather.11.cloned.1.call-update) | async-done | bytes 1179664 | tf_op jit(solution)/shard_map/all_gather | solution.py:220
  978.3 52.3 %all-gather.13.cloned.1.call-done = bf16[589824]{0:T(1024)(128)(2,1)} async-done(((bf16[18432]{0:T(1024)(128)(2,1)}), bf16[589824]{0:T(1024)(128)(2,1)}) %all-gather.13.cloned.1.call-update) | async-done | bytes 1179664 | tf_op jit(solution)/shard_map/all_gather | solution.py:223
  1033.9 62.4 %all-gather.15.cloned.1.call-done = bf16[2359296]{0:T(1024)(128)(2,1)} async-done(((bf16[73728]{0:T(1024)(128)(2,1)}), bf16[2359296]{0:T(1024)(128)(2,1)}) %all-gather.15.cloned.1.call-update) | async-done | bytes 4718608 | tf_op jit(solution)/shard_map/all_gather | solution.py:226
  1096.3 8.7 reshape.326
  1105.1 55.8 %all-gather.17.cloned.1.call-done = bf16[2359296]{0:T(1024)(128)(2,1)} async-done(((bf16[73728]{0:T(1024)(128)(2,1)}), bf16[2359296]{0:T(1024)(128)(2,1)}) %all-gather.17.cloned.1.call-update) | async-done | bytes 4718608 | tf_op jit(solution)/shard_map/all_gather | solution.py:229
  1160.9 10.0 reshape.328
  (227 shorter events, 178.1 us)
Async XLA Ops:
  13.6 9.1 copy-start.40
  13.7 32.6 %copy-start.9 = (bf16[300,768]{1,0:T(8,128)(2,1)}, bf16[300,768]{1,0:T(8,128)(2,1)S(1)}, u32[]{:S(2)}) copy-start(bf16[300,768]{1,0:T(8,128)(2,1)S(1)} %reshape.279) | copy-start | bytes 1382404
  16.3 26.5 %all-to-all-start = ((bf16[3,100,768]{1,0,2:T(4,128)(2,1)}), bf16[3,100,768]{1,0,2:T(4,128)(2,1)S(1)}, u32[]{:S(2)}, u32[]{:S(2)}) async-start(bf16[3,100,768]{1,0,2:T(4,128)(2,1)} %copy.96), calls=%async_computation | async-start | bytes 1572864 | tf_op jit(solution)/shard_map/all_to_all | solution.py:99
  25.9 44.3 %copy-start.38 = (s32[3,400]{1,0:T(4,128)S(1)}, s32[3,400]{1,0:T(4,128)}, u32[]{:S(2)}) copy-start(s32[3,400]{1,0:T(4,128)} %param.35) | copy-start | bytes 14404
  42.8 23.1 %all-to-all-start.1 = ((bf16[3,100,768]{1,0,2:T(4,128)(2,1)}), bf16[3,100,768]{1,0,2:T(4,128)(2,1)S(1)}, u32[]{:S(2)}, u32[]{:S(2)}) async-start(bf16[3,100,768]{1,0,2:T(4,128)(2,1)} %copy.99), calls=%async_computation.1 | async-start | bytes 1572864 | tf_op jit(solution)/shard_map/all_to_all | solution.py:97
  65.9 23.9 %all-to-all-start.2 = ((bf16[3,100,768]{1,0,2:T(4,128)(2,1)}), bf16[3,100,768]{1,0,2:T(4,128)(2,1)}, u32[]{:S(2)}, u32[]{:S(2)}) async-start(bf16[3,100,768]{1,0,2:T(4,128)(2,1)} %copy.102), calls=%async_computation.2 | async-start | bytes 1572864 | tf_op jit(solution)/shard_map/all_to_all | solution.py:98
  73.2 24.7 %copy-start.19 = (bf16[3,400,3,64]{1,3,2,0:T(8,128)(2,1)}, bf16[3,400,3,64]{1,3,2,0:T(8,128)(2,1)S(1)}, u32[]{:S(2)}) copy-start(bf16[3,400,3,64]{1,3,2,0:T(8,128)(2,1)S(1)} %reshape.281) | copy-start | bytes 1382404
  97.9 8.0 copy-start.39
  97.9 8.0 copy-start.42
  97.9 8.0 copy-start.43
  100.4 23.2 %copy-start.3 = (bf16[3,100,768]{2,1,0:T(8,128)(2,1)S(1)}, bf16[3,100,768]{2,1,0:T(8,128)(2,1)}, u32[]{:S(2)}) copy-start(bf16[3,100,768]{2,1,0:T(8,128)(2,1)} %param.18) | copy-start | bytes 1382404
  101.6 19.1 %all-to-all-start.3 = ((bf16[4,3,100,192]{2,3,1,0:T(8,128)(2,1)}), bf16[4,3,100,192]{2,3,1,0:T(8,128)(2,1)S(1)}, u32[]{:S(2)}, u32[]{:S(2)}) async-start(bf16[4,3,100,192]{2,3,1,0:T(8,128)(2,1)} %pad_maximum_fusion), calls=%async_computation.3 | async-start | bytes 1179648 | tf_op jit(solution)/shard_map/all_to_all | solution.py:113
  106.0 106.5 %copy-start.27 = (f32[3,3,400]{2,1,0:T(4,128)}, f32[3,3,400]{2,1,0:T(4,128)S(1)}, u32[]{:S(2)}) copy-start(f32[3,3,400]{2,1,0:T(4,128)S(1)} %log_add_fusion) | copy-start | bytes 43204
  125.7 43.6 %copy-start.7 = (f32[3,100,768]{2,1,0:T(8,128)}, f32[3,100,768]{2,1,0:T(8,128)S(1)}, u32[]{:S(2)}) copy-start(f32[3,100,768]{2,1,0:T(8,128)S(1)} %get-tuple-element.52) | copy-start | bytes 2764804
  170.8 10.6 copy-start.23
  176.8 26.1 %all-to-all-start.4 = ((bf16[3,100,768]{1,0,2:T(4,128)(2,1)}), bf16[3,100,768]{1,0,2:T(4,128)(2,1)}, u32[]{:S(2)}, u32[]{:S(2)}) async-start(bf16[3,100,768]{1,0,2:T(4,128)(2,1)} %copy.107), calls=%async_computation.4 | async-start | bytes 1572864 | tf_op jit(solution)/shard_map/all_to_all | solution.py:143
  181.4 14.3 %copy-start.16 = (bf16[3,100,4,192]{3,2,1,0:T(4,128)(2,1)S(1)}, bf16[3,100,4,192]{3,2,1,0:T(4,128)(2,1)}, u32[]{:S(2)}) copy-start(bf16[3,100,4,192]{3,2,1,0:T(4,128)(2,1)} %copy-done.15) | copy-start | bytes 1382404
  221.1 32.6 %all-to-all-start.5 = ((bf16[3,400,192]{2,0,1:T(4,128)(2,1)}), bf16[3,400,192]{2,0,1:T(4,128)(2,1)S(1)}, u32[]{:S(2)}, u32[]{:S(2)}) async-start(bf16[3,400,192]{2,0,1:T(4,128)(2,1)} %copy.111), calls=%async_computation.5 | async-start | bytes 1638400 | tf_op jit(solution)/shard_map/all_to_all | solution.py:171
  247.5 11.4 copy-start.28
  253.8 11.6 copy-start.11
  253.8 24.5 %all-to-all-start.6 = ((bf16[3,400,192]{2,0,1:T(4,128)(2,1)}), bf16[3,400,192]{2,0,1:T(4,128)(2,1)}, u32[]{:S(2)}, u32[]{:S(2)}) async-start(bf16[3,400,192]{2,0,1:T(4,128)(2,1)} %copy.115), calls=%async_computation.6 | async-start | bytes 1638400 | tf_op jit(solution)/shard_map/all_to_all | solution.py:172
  278.2 23.8 %all-to-all-start.7 = ((bf16[3,400,192]{2,0,1:T(4,128)(2,1)}), bf16[3,400,192]{2,0,1:T(4,128)(2,1)S(1)}, u32[]{:S(2)}, u32[]{:S(2)}) async-start(bf16[3,400,192]{2,0,1:T(4,128)(2,1)} %copy.119), calls=%async_computation.7 | async-start | bytes 1638400 | tf_op jit(solution)/shard_map/all_to_all | solution.py:173
  281.7 584.5 %all-gather.7.cloned.1.call-start = ((), (), s32[]{:S(2)}) async-start(), calls=%async_computation.8 | async-start | bytes 1216512 | tf_op jit(solution)/shard_map/all_gather | solution.py:214
  314.2 14.8 %copy-start.37 = (f32[768]{0:T(1024)S(1)}, f32[768]{0:T(1024)}, u32[]{:S(2)}) copy-start(f32[768]{0:T(1024)} %get-tuple-element.19) | copy-start | bytes 9220
  314.2 26.5 %copy-start.5 = (f32[768,768]{1,0:T(8,128)S(1)}, f32[768,768]{1,0:T(8,128)}, u32[]{:S(2)}) copy-start(f32[768,768]{1,0:T(8,128)} %fusion.75) | copy-start | bytes 7077892
  348.8 469.6 %copy-start.44 = (bf16[768]{0:T(1024)(128)(2,1)S(1)}, bf16[768]{0:T(1024)(128)(2,1)}, u32[]{:S(2)}) copy-start(bf16[768]{0:T(1024)(128)(2,1)} %param.34) | copy-start | bytes 4612
  809.2 12.0 %copy-start.8 = (f32[3,100,768]{2,1,0:T(8,128)S(1)}, f32[3,100,768]{2,1,0:T(8,128)}, u32[]{:S(2)}) copy-start(f32[3,100,768]{2,1,0:T(8,128)} %copy-done.7) | copy-start | bytes 2764804
  810.7 108.5 %all-gather.9.cloned.1.call-start = ((), (), s32[]{:S(2)}) async-start(), calls=%async_computation.9 | async-start | bytes 1216512 | tf_op jit(solution)/shard_map/all_gather | solution.py:217
  812.2 162.8 %all-gather.11.cloned.1.call-start = ((), (), s32[]{:S(2)}) async-start(), calls=%async_computation.10 | async-start | bytes 1216512 | tf_op jit(solution)/shard_map/all_gather | solution.py:220
  813.6 217.0 %all-gather.13.cloned.1.call-start = ((), (), s32[]{:S(2)}) async-start(), calls=%async_computation.11 | async-start | bytes 1216512 | tf_op jit(solution)/shard_map/all_gather | solution.py:223
  815.1 281.3 %all-gather.15.cloned.1.call-start = ((), (), s32[]{:S(2)}) async-start(), calls=%async_computation.12 | async-start | bytes 4866048 | tf_op jit(solution)/shard_map/all_gather | solution.py:226
  816.7 344.2 %all-gather.17.cloned.1.call-start = ((), (), s32[]{:S(2)}) async-start(), calls=%async_computation.13 | async-start | bytes 4866048 | tf_op jit(solution)/shard_map/all_gather | solution.py:229
  (27 other events, 106.9 us)
Sparse Core Ops, SparseCore 0:
  810.8 52.1 all-gather.6
  866.4 52.7 all-gather.8
  922.0 52.9 all-gather.10
  977.6 52.8 all-gather.12
  1033.8 62.5 all-gather.14
  1099.0 61.8 all-gather.16
